TPU v7x, 128 devices: a whole 4x4x4 slice. The times are simulated.
128 devices in a mesh: replica: 4 (over z), shard: 16 (over y, x_lo, core), tensor: 2 (over x_hi).
Axes of the slice: x: 4 (x_hi: 2, x_lo: 2; x = x_hi * 2 + x_lo), y: 4, z: 4, core: 2. Of those that a mesh axis runs over, the one named last changes fastest.
Arguments:
- trained_up: bfloat16 [4, 1024, 4096], P('replica', None, 'tensor'), may hold values from -6 to 6
- trained_down: bfloat16 [4, 4096, 1024], P('replica', 'tensor'), may hold values from -6 to 6
- trained_embed: bfloat16 [4, 32768, 1024], P('replica', ('shard', 'tensor')), may hold values from -6 to 6
- trained_norm: bfloat16 [4, 2, 1024], P('replica'), may hold values from 0.099609375 to 1.8984375
- master_up: float32 [1024, 4096], P(('replica', 'shard', 'tensor')), may hold values from -6 to 6
- moment_up: float32 [1024, 4096], P(('replica', 'shard', 'tensor')), may hold values from -4 to 4
- master_down: float32 [2, 2048, 1024], P('tensor', ('replica', 'shard')), may hold values from -6 to 6
- moment_down: float32 [2, 2048, 1024], P('tensor', ('replica', 'shard')), may hold values from -4 to 4
- master_embed: float32 [32, 1024, 1024], P(('shard', 'tensor'), 'replica'), may hold values from -6 to 6
- moment_embed: float32 [32, 1024, 64], P(('shard', 'tensor'), 'replica'), may hold values from -4 to 4
- master_norm: float32 [2, 1024], replicated, may hold values from 0.1 to 1.9
- moment_norm: float32 [2, 1024], replicated, may hold values from -2 to 2
- embed_basis: float32 [1024, 64], replicated, may hold values from -0.1875 to 0.1875
Outputs:
- recast_up: bfloat16 [1024, 4096], P(None, 'tensor')
- recast_down: bfloat16 [4096, 1024], P('tensor')
- recast_embed: bfloat16 [32768, 1024], P(('shard', 'tensor'))
- recast_norm: bfloat16 [2, 1024], replicated
- stored_up: float32 [1024, 4096], P(('replica', 'shard', 'tensor'))
- velocity_up: float32 [1024, 4096], P(('replica', 'shard', 'tensor'))
- stored_down: float32 [2, 2048, 1024], P('tensor', ('replica', 'shard'))
- velocity_down: float32 [2, 2048, 1024], P('tensor', ('replica', 'shard'))
- stored_embed: float32 [32, 1024, 1024], P(('shard', 'tensor'), 'replica')
- velocity_embed: float32 [32, 1024, 64], P(('shard', 'tensor'), 'replica')
- stored_norm: float32 [2, 1024], replicated
- velocity_norm: float32 [2, 1024], replicated
All inputs are finite; a program needn't handle non-finite values.
Results may differ from a plain program's by a relative error of at most 0.012.
Values may be sent and summed in bfloat16 or wider, within the bound.
A program may use at most 128 MiB of HBM per device.

v0:
```python
import jax
import jax.numpy as jnp
from jax import lax
from jax.sharding import PartitionSpec as P


def outer_step(master, moment, summed, groups):
    difference = master - summed / groups
    velocity = 0.5 * moment + difference
    return (master - 0.7 * (difference + 0.5 * velocity), velocity)


def body(
    trained_up,
    trained_down,
    trained_embed,
    trained_norm,
    master_up,
    moment_up,
    master_down,
    moment_down,
    master_embed,
    moment_embed,
    master_norm,
    moment_norm,
    embed_basis,
):
    replicas = lax.axis_size("replica")
    shards = lax.axis_size("shard")
    tensors = lax.axis_size("tensor")
    shard_pos = lax.axis_index("shard")
    width = embed_basis.shape[0]
    rows_up = master_up.shape[0]
    half_cols = trained_up.shape[2]
    rows_down = master_down.shape[1]
    up_blocks = trained_up[0].reshape(replicas, shards, tensors, rows_up, half_cols)
    up_own = lax.dynamic_index_in_dim(up_blocks, shard_pos, 1, keepdims=False)
    down_blocks = trained_down[0].reshape(replicas, shards, rows_down, width)
    down_own = lax.dynamic_index_in_dim(down_blocks, shard_pos, 1, keepdims=False)
    up_summed, down_summed = (
        lax.psum_scatter(
            up_own.astype(jnp.float32).astype(jnp.bfloat16),
            "replica",
            scatter_dimension=0,
            tiled=True,
        ).astype(jnp.float32),
        lax.psum_scatter(
            down_own.astype(jnp.float32).astype(jnp.bfloat16),
            "replica",
            scatter_dimension=0,
            tiled=True,
        ).astype(jnp.float32),
    )
    up_summed = lax.all_to_all(up_summed, "tensor", split_axis=1, concat_axis=3, tiled=True)
    stored_up, velocity_up = outer_step(
        master_up, moment_up, up_summed.reshape(rows_up, half_cols * tensors), replicas
    )
    stored_down, velocity_down = outer_step(master_down, moment_down, down_summed, replicas)
    norm_summed = lax.psum(trained_norm[0].astype(jnp.float32), "replica")
    stored_norm, velocity_norm = outer_step(master_norm, moment_norm, norm_summed, replicas)
    embed_own = master_embed[0]
    rows_embed = embed_own.shape[0]
    embed_terms = trained_embed[0].reshape(replicas, rows_embed, width).astype(jnp.float32)
    embed_summed = lax.psum_scatter(
        embed_terms.astype(jnp.bfloat16), "replica", scatter_dimension=0, tiled=True
    ).astype(jnp.float32)[0]
    coefficient = jnp.dot(
        embed_own - embed_summed / replicas, embed_basis, precision=lax.Precision.HIGHEST
    )
    velocity_rows = 0.5 * moment_embed[0] + coefficient
    stored_rows = embed_own - 0.7 * jnp.dot(
        coefficient + 0.5 * velocity_rows, embed_basis.T, precision=lax.Precision.HIGHEST
    )
    up_piece = lax.all_to_all(
        stored_up.astype(jnp.bfloat16), "tensor", split_axis=1, concat_axis=0, tiled=True
    )
    down_piece = stored_down[0].astype(jnp.bfloat16)
    recast_up, recast_down = (
        lax.all_gather(up_piece, ("replica", "shard"), axis=0, tiled=True),
        lax.all_gather(down_piece, ("replica", "shard"), axis=0, tiled=True),
    )
    recast_embed = lax.all_gather(stored_rows.astype(jnp.bfloat16), "replica", axis=0, tiled=True)
    return (
        recast_up,
        recast_down,
        recast_embed,
        stored_norm.astype(jnp.bfloat16),
        stored_up,
        velocity_up,
        stored_down,
        velocity_down,
        stored_rows[None],
        velocity_rows[None],
        stored_norm,
        velocity_norm,
    )


def solution(mesh):
    in_specs = (
        P("replica", None, "tensor"),
        P("replica", "tensor", None),
        P("replica", ("shard", "tensor"), None),
        P("replica", None, None),
        P(("replica", "shard", "tensor"), None),
        P(("replica", "shard", "tensor"), None),
        P("tensor", ("replica", "shard"), None),
        P("tensor", ("replica", "shard"), None),
        P(("shard", "tensor"), "replica", None),
        P(("shard", "tensor"), "replica", None),
        P(),
        P(),
        P(),
    )
    out_specs = (
        P(None, "tensor"),
        P("tensor", None),
        P(("shard", "tensor"), None),
        P(),
        P(("replica", "shard", "tensor"), None),
        P(("replica", "shard", "tensor"), None),
        P("tensor", ("replica", "shard"), None),
        P("tensor", ("replica", "shard"), None),
        P(("shard", "tensor"), "replica", None),
        P(("shard", "tensor"), "replica", None),
        P(),
        P(),
    )
    return jax.shard_map(body, mesh=mesh, in_specs=in_specs, out_specs=out_specs, check_vma=False)
```

profile of v0, /device:TPU:1, one launch (start us, length us, event | category | flops | bytes accessed | tf_op | source)
XLA Modules:
  0.0 376.6 jit_solution(8853071086595991756)
XLA Ops:
  7.3 0.7 reduce-scatter.6.cloned.1.call-update
  8.0 1.7 copy_bitcast_fusion
  9.8 1.7 dynamic-slice_bitcast_fusion
  11.6 32.1 %reduce-scatter.6.cloned.1.call-done = bf16[1,256,1024]{2,1,0:T(8,128)(2,1)} async-done(((bf16[4,256,1024]{2,1,0:T(8,128)(2,1)}), bf16[1,256,1024]{2,1,0:T(8,128)(2,1)}) %reduce-scatter.6.cloned.1.call-update) | async-done | bytes 524304 | tf_op jit(solution)/shard_map/reduce_scatter | solution.py:64
  43.6 2.2 fusion.1
  45.8 2.2 fusion.16
  48.1 0.6 dynamic-slice
  48.7 37.3 %all-reduce.3.cloned.1.call-done = bf16[4,2,8,2048]{3,2,0,1:T(8,128)(2,1)} async-done(((bf16[4,2,8,2048]{3,2,0,1:T(8,128)(2,1)}), bf16[4,2,8,2048]{3,2,0,1:T(8,128)(2,1)}) %all-reduce.3.cloned.1.call-update) | async-done | bytes 262160
  86.0 1.5 dynamic-slice_convert_fusion
  87.5 8.6 %all_to_all.28 = f32[1,2,8,2048]{3,2,0,1:T(8,128)S(1)} all-to-all(f32[1,2,8,2048]{3,2,0,1:T(8,128)S(1)} %dynamic-slice_convert_fusion), channel_id=1, replica_groups=mesh['replica'=4,'shard'=16,'tensor'=2] {'tensor'}, dimensions={1} | all-to-all | bytes 262144 | tf_op jit(solution)/shard_map/all_to_all | solution.py:54
  96.1 0.7 fusion.15
  96.9 7.5 %all_to_all.29 = bf16[8,2,2048]{2,0,1:T(8,128)(2,1)} all-to-all(bf16[8,2,2048]{2,0,1:T(8,128)(2,1)S(1)} %bitcast.53), channel_id=1, replica_groups=mesh['replica'=4,'shard'=16,'tensor'=2] {'tensor'}, dimensions={1} | all-to-all | bytes 131072 | tf_op jit(solution)/shard_map/all_to_all | solution.py:74
  104.4 5.8 %reduce-scatter.4.cloned.1.call-done = bf16[1,32,1024]{2,1,0:T(8,128)(2,1)} async-done(((bf16[4,32,1024]{2,1,0:T(8,128)(2,1)}), bf16[1,32,1024]{2,1,0:T(8,128)(2,1)}) %reduce-scatter.4.cloned.1.call-update) | async-done | bytes 65552 | tf_op jit(solution)/shard_map/reduce_scatter | solution.py:47
  110.3 1.6 fusion.14
  111.9 6.9 %psum.7 = f32[2,1024]{1,0:T(2,128)S(1)} all-reduce(f32[2,1024]{1,0:T(2,128)S(1)} %bitcast_convert_fusion), channel_id=1, replica_groups=mesh['replica'=4,'shard'=16,'tensor'=2] {'replica'}, use_global_device_ids=true, to_apply=%region_3.4 | all-reduce | flops 2048 | bytes 16384 | tf_op jit(solution)/shard_map/psum | solution.py:59
  118.9 0.6 fusion.13
  119.5 0.6 fusion.8
  120.2 25.0 %all-gather.7.cloned.1.call-done = bf16[1024,1024]{1,0:T(8,128)(2,1)} async-done(((bf16[256,1024]{1,0:T(8,128)(2,1)}), bf16[1024,1024]{1,0:T(8,128)(2,1)}) %all-gather.7.cloned.1.call-update) | async-done | bytes 2097168 | tf_op jit(solution)/shard_map/all_gather | solution.py:82
  145.2 108.0 %all-gather.5.cloned.1.call-done = bf16[1024,2048]{1,0:T(8,128)(2,1)} async-done(((bf16[16,2048]{1,0:T(8,128)(2,1)}), bf16[1024,2048]{1,0:T(8,128)(2,1)}) %all-gather.5.cloned.1.call-update) | async-done | bytes 4194320 | tf_op jit(solution)/shard_map/all_gather | solution.py:79
  253.2 107.3 %all-gather.9.cloned.1.call-done = bf16[1,2048,1024]{2,1,0:T(8,128)(2,1)} async-done(((bf16[1,32,1024]{2,1,0:T(8,128)(2,1)}), bf16[1,2048,1024]{2,1,0:T(8,128)(2,1)}) %all-gather.9.cloned.1.call-update) | async-done | bytes 4194320 | tf_op jit(solution)/shard_map/all_gather | solution.py:80
  360.4 4.9 %copy.39 = bf16[1024,2048]{1,0:T(8,128)(2,1)} copy(bf16[1024,2048]{1,0:T(8,128)(2,1)} %all-gather.5.cloned.1.call-done) | data formatting | bytes 8388608
  365.4 2.1 copy.40
  367.5 1.0 copy-done.3
  368.5 1.3 copy.41
  (38 shorter events, 0.4 us)
Async XLA Ops:
  7.2 36.5 %copy-start = (f32[1024,64]{0,1:T(8,128)S(1)}, f32[1024,64]{0,1:T(8,128)}, u32[]{:S(2)}) copy-start(f32[1024,64]{0,1:T(8,128)} %param.25) | copy-start | bytes 786436
  7.2 36.5 %copy-start.1 = (f32[1,256,1024]{2,1,0:T(8,128)S(1)}, f32[1,256,1024]{2,1,0:T(8,128)}, u32[]{:S(2)}) copy-start(f32[1,256,1024]{2,1,0:T(8,128)} %param.21) | copy-start | bytes 3145732
  7.2 38.6 %copy-start.4 = (f32[1,256,64]{1,2,0:T(8,128)S(1)}, f32[1,256,64]{1,2,0:T(8,128)}, u32[]{:S(2)}) copy-start(f32[1,256,64]{1,2,0:T(8,128)} %param.22) | copy-start | bytes 196612
  7.2 36.4 %reduce-scatter.6.cloned.1.call-start = ((), (), s32[]{:S(2)}) async-start(), calls=%async_computation.6 | async-start | bytes 2621440 | tf_op jit(solution)/shard_map/reduce_scatter | solution.py:64
  7.3 40.9 %copy-start.12 = (u32[128]{0:T(128)S(1)}, u32[128]{0:T(128)}, u32[]{:S(2)}) copy-start(u32[128]{0:T(128)} %constant.47) | copy-start | bytes 1540
  7.9 88.2 %copy-start.7 = (f32[8,4096]{1,0:T(8,128)S(1)}, f32[8,4096]{1,0:T(8,128)}, u32[]{:S(2)}) copy-start(f32[8,4096]{1,0:T(8,128)} %param.17) | copy-start | bytes 393220
  8.0 88.2 %copy-start.8 = (f32[8,4096]{1,0:T(8,128)S(1)}, f32[8,4096]{1,0:T(8,128)}, u32[]{:S(2)}) copy-start(f32[8,4096]{1,0:T(8,128)} %param.18) | copy-start | bytes 393220
  8.0 78.0 %all-reduce.3.cloned.1.call-start = ((), (), s32[]{:S(2)}) async-start(), calls=%async_computation.9 | async-start | bytes 524288
  9.7 100.6 %copy-start.5 = (f32[1,32,1024]{2,1,0:T(8,128)S(1)}, f32[1,32,1024]{2,1,0:T(8,128)}, u32[]{:S(2)}) copy-start(f32[1,32,1024]{2,1,0:T(8,128)} %param.19) | copy-start | bytes 393220
  9.7 100.6 %copy-start.6 = (f32[1,32,1024]{2,1,0:T(8,128)S(1)}, f32[1,32,1024]{2,1,0:T(8,128)}, u32[]{:S(2)}) copy-start(f32[1,32,1024]{2,1,0:T(8,128)} %param.20) | copy-start | bytes 393220
  9.7 100.6 %reduce-scatter.4.cloned.1.call-start = ((), (), s32[]{:S(2)}) async-start(), calls=%async_computation.5 | async-start | bytes 327680 | tf_op jit(solution)/shard_map/reduce_scatter | solution.py:47
  9.8 102.1 %copy-start.11 = (bf16[1,2,1024]{2,1,0:T(2,128)(2,1)S(1)}, bf16[1,2,1024]{2,1,0:T(2,128)(2,1)}, u32[]{:S(2)}) copy-start(bf16[1,2,1024]{2,1,0:T(2,128)(2,1)} %param.16) | copy-start | bytes 12292
  11.5 107.4 %copy-start.9 = (f32[2,1024]{1,0:T(2,128)S(1)}, f32[2,1024]{1,0:T(2,128)}, u32[]{:S(2)}) copy-start(f32[2,1024]{1,0:T(2,128)} %param.23) | copy-start | bytes 24580
  11.5 107.4 %copy-start.10 = (f32[2,1024]{1,0:T(2,128)S(1)}, f32[2,1024]{1,0:T(2,128)}, u32[]{:S(2)}) copy-start(f32[2,1024]{1,0:T(2,128)} %param.24) | copy-start | bytes 24580
  11.5 133.6 %all-gather.7.cloned.1.call-start = ((), (), s32[]{:S(2)}) async-start(), calls=%async_computation.7 | async-start | bytes 2621440 | tf_op jit(solution)/shard_map/all_gather | solution.py:82
  48.1 205.1 %all-gather.5.cloned.1.call-start = ((), (), s32[]{:S(2)}) async-start(), calls=%async_computation.4 | async-start | bytes 4259840 | tf_op jit(solution)/shard_map/all_gather | solution.py:79
  104.4 256.0 %all-gather.9.cloned.1.call-start = ((), (), s32[]{:S(2)}) async-start(), calls=%async_computation.8 | async-start | bytes 4259840 | tf_op jit(solution)/shard_map/all_gather | solution.py:80
  360.4 4.9 %copy-start.2 = (bf16[1,2048,1024]{2,1,0:T(8,128)(2,1)S(1)}, bf16[1,2048,1024]{2,1,0:T(8,128)(2,1)}, u32[]{:S(2)}) copy-start(bf16[1,2048,1024]{2,1,0:T(8,128)(2,1)} %all-gather.9.cloned.1.call-done) | copy-start | bytes 12582916
  365.4 3.1 copy-start.3
Sparse Core Ops, SparseCore 0:
  10.4 33.1 reduce-scatter.5
  46.7 39.3 all-reduce.2
  89.0 21.2 reduce-scatter.3
  112.5 32.6 all-gather.6
  146.9 106.2 all-gather.4
  255.4 104.9 all-gather.8
where the time goes:
time: 377 us
  waiting for transfers between devices  316 us (84%)
  blocking collectives  23 us (6%)
  between operations  14.3 us (4%)
  local copies, waits for them, and re-layouts  13.4 us (4%)
  other arithmetic  5.09 us (1%)
  matrix products  4.38 us (1%)
    all_gather x1, waiting for transfers between devices, body(): lax.all_gather(up_piece, ('replica', 'shard'), axis=0, tiled=True)  108 us
    all_gather x1, waiting for transfers between devices, body(): lax.all_gather(down_piece, ('replica', 'shard'), axis=0, tiled=True)  107 us
    unnamed x7, waiting for transfers between devices  38.1 us
    reduce_scatter x1, waiting for transfers between devices, body(): lax.psum_scatter(embed_terms.astype(jnp.bfloat16), 'replica', scatter_dim...  32.1 us
    all_gather x1, waiting for transfers between devices, body(): lax.all_gather(stored_rows.astype(jnp.bfloat16), 'replica', axis=0, tiled...  25 us
    unnamed x30, local copies, waits for them, and re-layouts  10 us
    all_to_all x1, blocking collectives, body(): lax.all_to_all(up_summed, 'tensor', split_axis=1, concat_axis=3, tiled=True)  8.59 us
  transfers between devices with their start and end apart: 6, of which 6 were waited for; matrix products, arithmetic and copies ran while one was open for 4% of the time, Pallas kernels for 0%

commit v1 on v0

--- a/solution.py
+++ b/solution.py
@@ -51,7 +51,16 @@
             tiled=True,
         ).astype(jnp.float32),
     )
-    up_summed = lax.all_to_all(up_summed, "tensor", split_axis=1, concat_axis=3, tiled=True)
+
+    def review_the_halves(incoming_x, comm_axis, array_axis, at_axis):
+        even = lax.axis_size(comm_axis)
+        big = jnp.split(incoming_x, even, axis=array_axis)
+        local_now = jnp.stack(big, 0)
+        x_new = lax.all_to_all(local_now, axis_name=comm_axis, concat_axis=0, split_axis=0)
+        block_out = jnp.concatenate(x_new, at_axis)
+        return block_out
+
+    up_summed = review_the_halves(up_summed, "tensor", 1, 3)
     stored_up, velocity_up = outer_step(
         master_up, moment_up, up_summed.reshape(rows_up, half_cols * tensors), replicas
     )

time: 377 us -> 356 us (0.944)
  waiting for transfers between devices: 316 us -> 295 us
    unnamed x7 -> x6, waiting for transfers between devices: 38.1 us -> 0.74 us
    reduce_scatter x0 -> x1, waiting for transfers between devices: none -> 21.8 us  [body(): lax.psum_scatter(up_own.astype(jnp.float32).astype(jnp.bfloat16), 'replic...]
    all_gather x1, waiting for transfers between devices: 25 us -> 8.26 us  [body(): lax.all_gather(stored_rows.astype(jnp.bfloat16), 'replica', axis=0, tiled...]
    reduce_scatter x1, waiting for transfers between devices: 5.85 us -> 16.7 us  [body(): lax.psum_scatter(down_own.astype(jnp.float32).astype(jnp.bfloat16), 'repl...]
    unnamed x30 -> x27, local copies, waits for them, and re-layouts: 10 us -> 9.42 us
  transfers between devices with their start and end apart: 6 -> 6, of which waited for: 6 -> 6; matrix products, arithmetic and copies ran while one was open for 4% -> 3% of each run, Pallas kernels for 0% -> 0%
where the time goes in v1:
time: 356 us; the launch traced here: 355 us
  waiting for transfers between devices  295 us (83%)
  blocking collectives  24.3 us (7%)
  between operations  14.3 us (4%)
  local copies, waits for them, and re-layouts  12.8 us (4%)
  other arithmetic  4.46 us (1%)
  matrix products  4.38 us (1%)
    all_gather x1, waiting for transfers between devices, body(): lax.all_gather(down_piece, ('replica', 'shard'), axis=0, tiled=True)  108 us
    all_gather x1, waiting for transfers between devices, body(): lax.all_gather(up_piece, ('replica', 'shard'), axis=0, tiled=True)  107 us
    reduce_scatter x1, waiting for transfers between devices, body(): lax.psum_scatter(embed_terms.astype(jnp.bfloat16), 'replica', scatter_dim...  32.1 us
    reduce_scatter x1, waiting for transfers between devices, body(): lax.psum_scatter(up_own.astype(jnp.float32).astype(jnp.bfloat16), 'replic...  21.8 us
    reduce_scatter x1, waiting for transfers between devices, body(): lax.psum_scatter(down_own.astype(jnp.float32).astype(jnp.bfloat16), 'repl...  16.7 us
    unnamed x27, local copies, waits for them, and re-layouts  9.42 us
    all_to_all x1, blocking collectives, review_the_halves(): lax.all_to_all(local_now, axis_name=comm_axis, concat_axis=0, split_axis=0)  8.6 us
    all_gather x1, waiting for transfers between devices, body(): lax.all_gather(stored_rows.astype(jnp.bfloat16), 'replica', axis=0, tiled...  8.26 us
  transfers between devices with their start and end apart: 6, of which 6 were waited for; matrix products, arithmetic and copies ran while one was open for 3% of the time, Pallas kernels for 0%

profile of v1, /device:TPU:1, one launch (start us, length us, event | category | flops | bytes accessed | tf_op | source)
XLA Modules:
  0.0 355.1 jit_solution(1200229312679613573)
XLA Ops:
  7.3 0.7 reduce-scatter.8.cloned.1.call-update
  8.0 1.7 dynamic-slice_bitcast_fusion
  9.7 0.0 reduce-scatter.4.cloned.1.call-start
  9.8 1.7 dynamic-slice_bitcast_fusion.1
  11.6 32.1 %reduce-scatter.8.cloned.1.call-done = bf16[1,256,1024]{2,1,0:T(8,128)(2,1)} async-done(((bf16[4,256,1024]{2,1,0:T(8,128)(2,1)}), bf16[1,256,1024]{2,1,0:T(8,128)(2,1)}) %reduce-scatter.8.cloned.1.call-update) | async-done | bytes 524304 | tf_op jit(solution)/shard_map/reduce_scatter | solution.py:73
  43.6 2.2 fusion.1
  45.8 2.2 fusion.16
  48.1 16.7 %reduce-scatter.6.cloned.1.call-done = bf16[1,32,1024]{2,1,0:T(8,128)(2,1)} async-done(((bf16[4,32,1024]{2,1,0:T(8,128)(2,1)}), bf16[1,32,1024]{2,1,0:T(8,128)(2,1)}) %reduce-scatter.6.cloned.1.call-update) | async-done | bytes 65552 | tf_op jit(solution)/shard_map/reduce_scatter | solution.py:47
  64.9 1.6 fusion.14
  66.5 21.8 %reduce-scatter.4.cloned.1.call-done = bf16[1,2,8,2048]{3,2,1,0:T(8,128)(2,1)} async-done(((bf16[4,2,8,2048]{3,2,1,0:T(8,128)(2,1)}), bf16[1,2,8,2048]{3,2,1,0:T(8,128)(2,1)}) %reduce-scatter.4.cloned.1.call-update) | async-done | bytes 65552 | tf_op jit(solution)/shard_map/reduce_scatter | solution.py:41
  88.3 0.8 convert_element_type.36
  89.2 8.6 %all_to_all.24 = f32[2,1,1,8,2048]{4,3,2,1,0:T(8,128)S(1)} all-to-all(f32[2,1,1,8,2048]{4,3,2,1,0:T(8,128)S(1)} %pad_maximum_fusion), channel_id=1, replica_groups=mesh['replica'=4,'shard'=16,'tensor'=2] {'tensor'}, dimensions={0} | all-to-all | bytes 262144 | tf_op jit(solution)/shard_map/all_to_all | solution.py:59
  97.8 0.7 fusion.15
  98.6 7.5 %all_to_all.25 = bf16[8,2,2048]{2,0,1:T(8,128)(2,1)} all-to-all(bf16[8,2,2048]{2,0,1:T(8,128)(2,1)S(1)} %bitcast.54), channel_id=1, replica_groups=mesh['replica'=4,'shard'=16,'tensor'=2] {'tensor'}, dimensions={1} | all-to-all | bytes 131072 | tf_op jit(solution)/shard_map/all_to_all | solution.py:83
  106.1 8.2 %psum.7 = f32[2,1024]{1,0:T(2,128)S(1)} all-reduce(f32[2,1024]{1,0:T(2,128)S(1)} %bitcast_convert_fusion), channel_id=1, replica_groups=mesh['replica'=4,'shard'=16,'tensor'=2] {'replica'}, use_global_device_ids=true, to_apply=%region_3.4 | all-reduce | flops 2048 | bytes 16384 | tf_op jit(solution)/shard_map/psum | solution.py:68
  114.3 0.6 fusion.13
  114.9 0.6 fusion.8
  115.5 8.3 %all-gather.7.cloned.1.call-done = bf16[1024,1024]{1,0:T(8,128)(2,1)} async-done(((bf16[256,1024]{1,0:T(8,128)(2,1)}), bf16[1024,1024]{1,0:T(8,128)(2,1)}) %all-gather.7.cloned.1.call-update) | async-done | bytes 2097168 | tf_op jit(solution)/shard_map/all_gather | solution.py:91
  123.8 108.4 %all-gather.9.cloned.1.call-done = bf16[1,2048,1024]{2,1,0:T(8,128)(2,1)} async-done(((bf16[1,32,1024]{2,1,0:T(8,128)(2,1)}), bf16[1,2048,1024]{2,1,0:T(8,128)(2,1)}) %all-gather.9.cloned.1.call-update) | async-done | bytes 4194320 | tf_op jit(solution)/shard_map/all_gather | solution.py:89
  232.2 106.7 %all-gather.5.cloned.1.call-done = bf16[1024,2048]{1,0:T(8,128)(2,1)} async-done(((bf16[16,2048]{1,0:T(8,128)(2,1)}), bf16[1024,2048]{1,0:T(8,128)(2,1)}) %all-gather.5.cloned.1.call-update) | async-done | bytes 4194320 | tf_op jit(solution)/shard_map/all_gather | solution.py:88
  338.9 4.9 %copy.34 = bf16[1024,2048]{1,0:T(8,128)(2,1)} copy(bf16[1024,2048]{1,0:T(8,128)(2,1)} %all-gather.5.cloned.1.call-done) | data formatting | bytes 8388608
  343.8 2.1 copy.35
  346.0 1.0 copy-done.3
  346.9 1.3 copy.36
  (37 shorter events, 0.4 us)
Async XLA Ops:
  7.2 36.5 %copy-start = (f32[1024,64]{0,1:T(8,128)S(1)}, f32[1024,64]{0,1:T(8,128)}, u32[]{:S(2)}) copy-start(f32[1024,64]{0,1:T(8,128)} %param.25) | copy-start | bytes 786436
  7.2 36.5 %copy-start.1 = (f32[1,256,1024]{2,1,0:T(8,128)S(1)}, f32[1,256,1024]{2,1,0:T(8,128)}, u32[]{:S(2)}) copy-start(f32[1,256,1024]{2,1,0:T(8,128)} %param.21) | copy-start | bytes 3145732
  7.2 38.6 %copy-start.4 = (f32[1,256,64]{1,2,0:T(8,128)S(1)}, f32[1,256,64]{1,2,0:T(8,128)}, u32[]{:S(2)}) copy-start(f32[1,256,64]{1,2,0:T(8,128)} %param.22) | copy-start | bytes 196612
  7.2 36.4 %reduce-scatter.8.cloned.1.call-start = ((), (), s32[]{:S(2)}) async-start(), calls=%async_computation.8 | async-start | bytes 2621440 | tf_op jit(solution)/shard_map/reduce_scatter | solution.py:73
  7.3 57.6 %copy-start.5 = (f32[1,32,1024]{2,1,0:T(8,128)S(1)}, f32[1,32,1024]{2,1,0:T(8,128)}, u32[]{:S(2)}) copy-start(f32[1,32,1024]{2,1,0:T(8,128)} %param.19) | copy-start | bytes 393220
  7.3 57.6 %copy-start.6 = (f32[1,32,1024]{2,1,0:T(8,128)S(1)}, f32[1,32,1024]{2,1,0:T(8,128)}, u32[]{:S(2)}) copy-start(f32[1,32,1024]{2,1,0:T(8,128)} %param.20) | copy-start | bytes 393220
  7.9 56.9 %reduce-scatter.6.cloned.1.call-start = ((), (), s32[]{:S(2)}) async-start(), calls=%async_computation.7 | async-start | bytes 327680 | tf_op jit(solution)/shard_map/reduce_scatter | solution.py:47
  9.7 88.1 %copy-start.7 = (f32[8,4096]{1,0:T(8,128)S(1)}, f32[8,4096]{1,0:T(8,128)}, u32[]{:S(2)}) copy-start(f32[8,4096]{1,0:T(8,128)} %param.17) | copy-start | bytes 393220
  9.7 88.1 %copy-start.8 = (f32[8,4096]{1,0:T(8,128)S(1)}, f32[8,4096]{1,0:T(8,128)}, u32[]{:S(2)}) copy-start(f32[8,4096]{1,0:T(8,128)} %param.18) | copy-start | bytes 393220
  9.7 78.6 %reduce-scatter.4.cloned.1.call-start = ((), (), s32[]{:S(2)}) async-start(), calls=%async_computation.5 | async-start | bytes 327680 | tf_op jit(solution)/shard_map/reduce_scatter | solution.py:41
  11.5 94.6 %copy-start.11 = (bf16[1,2,1024]{2,1,0:T(2,128)(2,1)S(1)}, bf16[1,2,1024]{2,1,0:T(2,128)(2,1)}, u32[]{:S(2)}) copy-start(bf16[1,2,1024]{2,1,0:T(2,128)(2,1)} %param.16) | copy-start | bytes 12292
  11.5 102.8 %copy-start.9 = (f32[2,1024]{1,0:T(2,128)S(1)}, f32[2,1024]{1,0:T(2,128)}, u32[]{:S(2)}) copy-start(f32[2,1024]{1,0:T(2,128)} %param.23) | copy-start | bytes 24580
  11.5 102.8 %copy-start.10 = (f32[2,1024]{1,0:T(2,128)S(1)}, f32[2,1024]{1,0:T(2,128)}, u32[]{:S(2)}) copy-start(f32[2,1024]{1,0:T(2,128)} %param.24) | copy-start | bytes 24580
  11.5 112.3 %all-gather.7.cloned.1.call-start = ((), (), s32[]{:S(2)}) async-start(), calls=%async_computation.9 | async-start | bytes 2621440 | tf_op jit(solution)/shard_map/all_gather | solution.py:91
  48.1 184.1 %all-gather.9.cloned.1.call-start = ((), (), s32[]{:S(2)}) async-start(), calls=%async_computation.10 | async-start | bytes 4259840 | tf_op jit(solution)/shard_map/all_gather | solution.py:89
  66.5 272.4 %all-gather.5.cloned.1.call-start = ((), (), s32[]{:S(2)}) async-start(), calls=%async_computation.6 | async-start | bytes 4259840 | tf_op jit(solution)/shard_map/all_gather | solution.py:88
  338.9 4.9 %copy-start.2 = (bf16[1,2048,1024]{2,1,0:T(8,128)(2,1)S(1)}, bf16[1,2048,1024]{2,1,0:T(8,128)(2,1)}, u32[]{:S(2)}) copy-start(bf16[1,2048,1024]{2,1,0:T(8,128)(2,1)} %all-gather.9.cloned.1.call-done) | copy-start | bytes 12582916
  343.8 3.1 copy-start.3
Sparse Core Ops, SparseCore 0:
  10.4 33.1 reduce-scatter.7
  46.7 18.1 reduce-scatter.5
  67.8 20.4 reduce-scatter.3
  90.5 33.2 all-gather.6
  126.1 106.0 all-gather.8
  233.9 104.9 all-gather.4
